TPU v7x, 32 devices: a whole 2x2x4 slice. The times are simulated.
32 devices in a mesh: lon: 8 (over z, x), lat: 4 (over y, core).
Axes of the slice: x: 2, y: 2, z: 4, core: 2. Of those that a mesh axis runs over, the one named last changes fastest.
Arguments:
- inputs: bfloat16 [256, 32, 2048], P(None, 'lat', 'lon'), may hold values from -6 to 6
- cotangent: bfloat16 [256, 32, 2048], P(None, 'lat', 'lon'), may hold values from -6 to 6
- mixing: bfloat16 [9, 256, 256], replicated, may hold values from -0.125 to 0.125
- filters: bfloat16 [9, 32, 3, 33], P(None, 'lat'), may hold values from -0.8984375 to 0.8984375
- support: int32 [32], P('lat'), may hold values from 1 to 16, as said below
Outputs:
- input_grad: bfloat16 [256, 32, 2048], P(None, 'lat', 'lon')
- weight_grad: float32 [9, 256, 256], replicated
Inputs may be any that keep to these rules, and one draw needn't show every extreme that they name: support[i] is the widest longitude offset, in cells, reached by the filter of latitude row i.
All inputs are finite; a program needn't handle non-finite values.
Results may differ from a plain program's by a relative error of at most 0.0051.
Values may be sent and summed in bfloat16 or wider, within the bound.
A program may use at most 192 MiB of HBM per device.

v0:
```python
import math
import jax
import jax.numpy as jnp
from jax import lax
from jax.sharding import PartitionSpec as P

LAT_REACH = 1
LON_REACH = 16


def with_halo(cells, sides, width, closed):
    for axis, dim in sides:
        count = lax.axis_size(axis)
        ends = count if closed else count - 1
        head = lax.slice_in_dim(cells, 0, width, axis=dim)
        tail = lax.slice_in_dim(cells, cells.shape[dim] - width, cells.shape[dim], axis=dim)
        cells = jnp.concatenate(
            [
                lax.ppermute(tail, axis, [(i, (i + 1) % count) for i in range(ends)]),
                cells,
                lax.ppermute(head, axis, [((i + 1) % count, i) for i in range(ends)]),
            ],
            axis=dim,
        )
    return cells


def spread_block(source, coef_source, row_first, rows, col_first, cols):
    kernels = coef_source.shape[0]
    chans = source.shape[0]
    span = LON_REACH
    reach = LAT_REACH
    tap_count = 2 * span + 1
    window = cols + 2 * span
    tap_axis = jnp.arange(tap_count, dtype=jnp.int32)[:, None, None]
    wide_axis = jnp.arange(window, dtype=jnp.int32)[None, :, None]
    cell_axis = jnp.arange(cols, dtype=jnp.int32)[None, None, :]
    selector = (cell_axis + 2 * span - wide_axis == tap_axis).astype(jnp.bfloat16)
    total = jnp.zeros((kernels, chans, rows, cols), jnp.float32)
    for offset in range(2 * reach + 1):
        start = row_first + 2 * reach - offset
        rows_in = source[:, start : start + rows, col_first : col_first + window]
        part_coefs = coef_source[:, start : start + rows, offset, :]
        tiles = jnp.einsum(
            "bpq,kib->kipq", selector, part_coefs, preferred_element_type=jnp.float32
        ).astype(jnp.bfloat16)
        total = total + jnp.einsum(
            "oip,kipq->koiq", rows_in, tiles, preferred_element_type=jnp.float32
        )
    return total.astype(jnp.bfloat16)


def local(inputs, cotangent, mixing, filters, support):
    chans, lat_rows, lon_cols = inputs.shape
    span = LON_REACH
    reach = LAT_REACH
    tap_count = 2 * span + 1
    offsets = jnp.arange(tap_count, dtype=jnp.int32) - span
    keep = (jnp.abs(offsets)[None, :] <= support[:, None]).astype(jnp.bfloat16)
    coefs = filters * keep[None, :, None, :]
    widened = with_halo(cotangent, (("lon", 2),), span, True)
    padded = with_halo(widened, (("lat", 1),), reach, False)
    coef_pad = with_halo(coefs, (("lat", 1),), reach, False)
    spread = spread_block(padded, coef_pad, 0, lat_rows, 0, lon_cols)
    local_grad = jnp.einsum("koiq,ciq->koc", spread, inputs, preferred_element_type=jnp.float32)
    total_cells = lat_rows * lax.axis_size("lat") * lon_cols * lax.axis_size("lon")
    weight_grad = lax.psum(local_grad, ("lon", "lat")) * (1.0 / math.sqrt(total_cells))
    input_grad = jnp.einsum(
        "koc,koiq->ciq", mixing, spread, preferred_element_type=jnp.float32
    ).astype(jnp.bfloat16)
    return (input_grad, weight_grad)


def solution(mesh):
    return jax.shard_map(
        local,
        mesh=mesh,
        in_specs=(
            P(None, "lat", "lon"),
            P(None, "lat", "lon"),
            P(),
            P(None, "lat", None, None),
            P("lat"),
        ),
        out_specs=(P(None, "lat", "lon"), P()),
        check_vma=False,
    )
```

profile of v0, /device:TPU:0, one launch (start us, length us, event | category | flops | bytes accessed | tf_op | source)
XLA Modules:
  0.0 247.0 jit_solution(17493707170582099157)
XLA Ops:
  7.2 0.0 copy-start
  7.2 0.0 copy-start.2
  7.2 0.0 copy-start.1
  7.2 0.0 all-reduce.2.cloned.1.call-start
  7.2 1.7 copy.7
  9.0 3.0 %collective-permute-start.1 = (bf16[256,8,16]{0,2,1:T(8,128)(2,1)S(1)}, bf16[256,8,16]{0,2,1:T(8,128)(2,1)S(1)}, u32[]{:S(2)}, u32[]{:S(2)}) collective-permute-start(bf16[256,8,16]{0,2,1:T(8,128)(2,1)S(1)} %get-tuple-element.6), channel_id=1, source_target_pairs={{0,4},{4,8},{8,12},{12,16},{16,20},{20,24},{24,28},{28,0},{1,5},{5... | collective-permute-start | bytes 196616 | tf_op jit(solution)/shard_map/ppermute | solution.py:19
  12.0 3.1 %collective-permute-start.2 = (bf16[256,8,16]{0,2,1:T(8,128)(2,1)S(1)}, bf16[256,8,16]{0,2,1:T(8,128)(2,1)S(1)}, u32[]{:S(2)}, u32[]{:S(2)}) collective-permute-start(bf16[256,8,16]{0,2,1:T(8,128)(2,1)S(1)} %get-tuple-element.7), channel_id=1, source_target_pairs={{4,0},{8,4},{12,8},{16,12},{20,16},{24,20},{28,24},{0,28},{5,1},{9... | collective-permute-start | bytes 196616 | tf_op jit(solution)/shard_map/ppermute | solution.py:21
  15.1 0.0 copy-done.2
  15.1 0.1 compare_convert_fusion
  15.2 0.0 copy-done.1
  15.2 1.3 collective-permute-start
  16.5 3.0 %collective-permute-start.4 = (bf16[9,1,3,33]{3,1,2,0:T(2,128)(2,1)S(1)}, bf16[9,1,3,33]{3,1,2,0:T(2,128)(2,1)S(1)}, u32[]{:S(2)}, u32[]{:S(2)}) collective-permute-start(bf16[9,1,3,33]{3,1,2,0:T(2,128)(2,1)S(1)} %get-tuple-element.8), channel_id=1, source_target_pairs={{0,1},{1,2},{2,3},{4,5},{5,6},{6,7},{8,9},{9,10},{10,11},{12,13},{... | collective-permute-start | bytes 5354 | tf_op jit(solution)/shard_map/ppermute | solution.py:19
  19.6 1.3 fusion.3
  20.9 6.6 %fusion.7 = bf16[9,8,288,256]{3,1,2,0:T(8,128)(2,1)} fusion(pred[33,288,256,1]{2,1,0,3:T(32,128)(4,1)S(1)} %fusion.3, bf16[9,8,3,33]{3,1,2,0:T(8,128)(2,1)S(1)} %broadcast_multiply_fusion.1), kind=kOutput, calls=%fused_computation.12 | convolution fusion | flops 350355456 | bytes 13068288 | tf_op jit(solution)/shard_map/bpq,kib->kipq/dot_general | solution.py:44
  27.5 0.0 collective-permute-done
  27.5 6.6 %fusion.9 = bf16[9,8,288,256]{3,1,2,0:T(8,128)(2,1)} fusion(pred[33,288,256,1]{2,1,0,3:T(32,128)(4,1)S(1)} %fusion.3, bf16[9,1,3,33]{3,1,2,0:T(2,128)(2,1)S(1)} %collective-permute-done, bf16[9,8,3,33]{3,1,2,0:T(8,128)(2,1)S(1)} %broadcast_multiply_fusion.1), kind=kOutput, calls=%fused_computation.14 | convolution fusion | flops 350364960 | bytes 13065894 | tf_op jit(solution)/shard_map/bpq,kib->kipq/dot_general | solution.py:44
  34.1 0.0 collective-permute-done.4
  34.1 6.6 %fusion.5 = bf16[9,8,288,256]{3,1,2,0:T(8,128)(2,1)} fusion(pred[33,288,256,1]{2,1,0,3:T(32,128)(4,1)S(1)} %fusion.3, bf16[9,8,3,33]{3,1,2,0:T(8,128)(2,1)S(1)} %broadcast_multiply_fusion.1, bf16[9,1,3,33]{3,1,2,0:T(2,128)(2,1)S(1)} %collective-permute-done.4), kind=kOutput, calls=%fused_computation.10 | convolution fusion | flops 350364960 | bytes 13065894 | tf_op jit(solution)/shard_map/bpq,kib->kipq/dot_general | solution.py:44
  40.7 0.0 collective-permute-done.1
  40.7 0.0 collective-permute-done.2
  40.7 0.1 pad_maximum_fusion.10
  40.8 0.0 slice-start
  40.8 0.7 fusion.31
  41.5 1.4 collective-permute-start.3
  42.9 0.0 slice-start.1
  43.0 0.0 slice-start.2
  43.0 4.7 %collective-permute-start.5 = (bf16[256,1,288]{0,2,1:T(8,128)(2,1)}, bf16[256,1,288]{0,2,1:T(8,128)(2,1)}, u32[]{:S(2)}, u32[]{:S(2)}) collective-permute-start(bf16[256,1,288]{0,2,1:T(8,128)(2,1)} %get-tuple-element.4), channel_id=1, source_target_pairs={{0,1},{1,2},{2,3},{4,5},{5,6},{6,7},{8,9},{9,10},{10,11},{12,13},{... | collective-permute-start | bytes 442376 | tf_op jit(solution)/shard_map/ppermute | solution.py:19
  47.7 12.9 %fusion.1 = f32[8,9,256,256]{3,2,1,0:T(8,128)} fusion(bf16[9,8,288,256]{3,1,2,0:T(8,128)(2,1)} %fusion.7, bf16[256,8,16]{0,2,1:T(8,128)(2,1)S(1)} %collective-permute-done.2, bf16[256,8,256]{0,2,1:T(8,128)(2,1)S(1)} %copy.7, bf16[256,8,16]{0,2,1:T(8,128)(2,1)S(1)} %collective-permute-done.1), kind=kOutput, calls=%fused_computation.5 | convolution fusion | flops 2721447936 | bytes 30670848 | tf_op jit(solution)/shard_map/oip,kipq->koiq/dot_general | solution.py:47
  60.6 0.0 collective-permute-done.3
  60.6 0.0 slice-done
  60.6 0.0 slice-done.1
  60.6 0.0 slice-done.2
  60.6 12.4 %fusion = f32[8,9,256,256]{3,2,1,0:T(8,128)} fusion(bf16[9,8,288,256]{3,1,2,0:T(8,128)(2,1)S(1)} %bitcast.53, bf16[256,1,288]{0,2,1:T(8,128)(2,1)} %collective-permute-done.3, bf16[256,8,16]{0,2,1:T(8,128)(2,1)S(1)} %collective-permute-done.2, bf16[256,8,256]{0,2,1:T(8,128)(2,1)S(1)} %copy.7, bf16[256,8,16]{0,2,1:T(8,128)(2,1)S(1)} %collective-permute-done.1), kind=kOutput, calls=%fused_computation.4 | convolution fusion | flops 2722627584 | bytes 30818304 | tf_op jit(solution)/shard_map/oip,kipq->koiq/dot_general | solution.py:47
  73.0 0.0 copy-start.3
  73.0 0.0 collective-permute-done.5
  73.0 21.8 %fusion.4 = bf16[9,256,8,256]{1,3,0,2:T(8,128)(2,1)} fusion(f32[8,9,256,256]{3,2,1,0:T(8,128)} %fusion, f32[8,9,256,256]{3,2,1,0:T(8,128)} %fusion.1, bf16[9,8,288,256]{3,1,2,0:T(8,128)(2,1)} %fusion.5, bf16[256,1,288]{0,2,1:T(8,128)(2,1)} %collective-permute-done.5, bf16[256,8,16]{0,2,1:T(8,128)(2,1)S(1)} %collective-permute-done.2, ...), kind=kOutput, calls=%fused_computation.9 | convolution fusion | flops 2736783360 | bytes 59129856 | tf_op jit(solution)/shard_map/oip,kipq->koiq/dot_general | solution.py:47
  94.8 0.0 copy-done.3
  94.8 7.8 %convolution_bitcast_fusion = f32[9,256,256]{2,1,0:T(8,128)} fusion(bf16[9,256,8,256]{1,3,0,2:T(8,128)(2,1)} %fusion.4, bf16[256,8,256,1]{2,1,0,3:T(8,128)(2,1)S(1)} %bitcast.54), kind=kOutput, calls=%fused_computation.17 | convolution fusion | flops 2415919104 | bytes 12845056 | tf_op jit(solution)/shard_map/koiq,ciq->koc/dot_general | solution.py:65
  102.6 0.0 all-reduce.2.cloned.1.call-update
  102.6 0.0 copy-done
  102.6 6.3 %fusion.11 = bf16[256,8,256]{0,2,1:T(8,128)(2,1)S(1)} fusion(bf16[9,256,8,256]{1,3,0,2:T(8,128)(2,1)} %fusion.4, bf16[9,256,256]{2,1,0:T(8,128)(2,1)S(1)} %copy-done), kind=kOutput, calls=%fused_computation.18 | convolution fusion | flops 2416443392 | bytes 11665408 | tf_op jit(solution)/shard_map/koc,koiq->ciq/dot_general | solution.py:68
  109.0 1.8 copy.12
  110.8 126.1 %all-reduce.2.cloned.1.call-done = f32[9,256,256]{2,1,0:T(8,128)} async-done(((f32[9,256,256]{2,1,0:T(8,128)}), f32[9,256,256]{2,1,0:T(8,128)}) %all-reduce.2.cloned.1.call-update) | async-done | bytes 2359312 | tf_op jit(solution)/shard_map/psum | solution.py:67
  236.8 3.3 %broadcast_multiply_fusion = f32[9,256,256]{2,1,0:T(8,128)} fusion(f32[9,256,256]{2,1,0:T(8,128)} %all-reduce.2.cloned.1.call-done), kind=kLoop, calls=%fused_computation.32 | loop fusion | flops 589824 | bytes 4718592 | tf_op jit(solution)/shard_map/mul | solution.py:67
  (7 shorter events, 0.1 us)
Async XLA Ops:
  7.2 95.5 %copy-start = (bf16[9,256,256]{2,1,0:T(8,128)(2,1)S(1)}, bf16[9,256,256]{2,1,0:T(8,128)(2,1)}, u32[]{:S(2)}) copy-start(bf16[9,256,256]{2,1,0:T(8,128)(2,1)} %param.7) | copy-start | bytes 3538948
  7.2 7.9 %copy-start.2 = (s32[8]{0:T(128)S(1)}, s32[8]{0:T(128)}, u32[]{:S(2)}) copy-start(s32[8]{0:T(128)} %param.9) | copy-start | bytes 100
  7.2 8.0 %copy-start.1 = (bf16[9,8,3,33]{3,1,2,0:T(8,128)(2,1)S(1)}, bf16[9,8,3,33]{3,1,2,0:T(8,128)(2,1)}, u32[]{:S(2)}) copy-start(bf16[9,8,3,33]{3,1,2,0:T(8,128)(2,1)} %param.8) | copy-start | bytes 42772
  7.2 229.6 %all-reduce.2.cloned.1.call-start = ((), (), s32[]{:S(2)}) async-start(), calls=%async_computation | async-start | bytes 4718592 | tf_op jit(solution)/shard_map/psum | solution.py:67
  9.0 31.7 %collective-permute-start.1 = (bf16[256,8,16]{0,2,1:T(8,128)(2,1)S(1)}, bf16[256,8,16]{0,2,1:T(8,128)(2,1)S(1)}, u32[]{:S(2)}, u32[]{:S(2)}) collective-permute-start(bf16[256,8,16]{0,2,1:T(8,128)(2,1)S(1)} %get-tuple-element.6), channel_id=1, source_target_pairs={{0,4},{4,8},{8,12},{12,16},{16,20},{20,24},{24,28},{28,0},{1,5},{5... | collective-permute-start | bytes 196616 | tf_op jit(solution)/shard_map/ppermute | solution.py:19
  12.0 28.7 %collective-permute-start.2 = (bf16[256,8,16]{0,2,1:T(8,128)(2,1)S(1)}, bf16[256,8,16]{0,2,1:T(8,128)(2,1)S(1)}, u32[]{:S(2)}, u32[]{:S(2)}) collective-permute-start(bf16[256,8,16]{0,2,1:T(8,128)(2,1)S(1)} %get-tuple-element.7), channel_id=1, source_target_pairs={{4,0},{8,4},{12,8},{16,12},{20,16},{24,20},{28,24},{0,28},{5,1},{9... | collective-permute-start | bytes 196616 | tf_op jit(solution)/shard_map/ppermute | solution.py:21
  15.2 12.3 %collective-permute-start = (bf16[9,1,3,33]{3,1,2,0:T(2,128)(2,1)S(1)}, bf16[9,1,3,33]{3,1,2,0:T(2,128)(2,1)S(1)}, u32[]{:S(2)}, u32[]{:S(2)}) collective-permute-start(bf16[9,1,3,33]{3,1,2,0:T(2,128)(2,1)S(1)} %get-tuple-element.9), channel_id=1, source_target_pairs={{1,0},{2,1},{3,2},{5,4},{6,5},{7,6},{9,8},{10,9},{11,10},{13,12},{... | collective-permute-start | bytes 5354 | tf_op jit(solution)/shard_map/ppermute | solution.py:21
  16.5 17.5 %collective-permute-start.4 = (bf16[9,1,3,33]{3,1,2,0:T(2,128)(2,1)S(1)}, bf16[9,1,3,33]{3,1,2,0:T(2,128)(2,1)S(1)}, u32[]{:S(2)}, u32[]{:S(2)}) collective-permute-start(bf16[9,1,3,33]{3,1,2,0:T(2,128)(2,1)S(1)} %get-tuple-element.8), channel_id=1, source_target_pairs={{0,1},{1,2},{2,3},{4,5},{5,6},{6,7},{8,9},{9,10},{10,11},{12,13},{... | collective-permute-start | bytes 5354 | tf_op jit(solution)/shard_map/ppermute | solution.py:19
  40.8 19.8 %slice-start = ((s8[10616832]{0:T(1024)(128)(4,1)}), s8[4194304]{0:T(1024)(128)(4,1)S(1)}, s32[]{:S(2)}) async-start(s8[10616832]{0:T(1024)(128)(4,1)} %bitcast.52), calls=%async_computation.1 | async-start | bytes 8388608
  41.5 19.1 %collective-permute-start.3 = (bf16[256,1,288]{0,2,1:T(8,128)(2,1)}, bf16[256,1,288]{0,2,1:T(8,128)(2,1)}, u32[]{:S(2)}, u32[]{:S(2)}) collective-permute-start(bf16[256,1,288]{0,2,1:T(8,128)(2,1)} %get-tuple-element.5), channel_id=1, source_target_pairs={{1,0},{2,1},{3,2},{5,4},{6,5},{7,6},{9,8},{10,9},{11,10},{13,12},{... | collective-permute-start | bytes 442376 | tf_op jit(solution)/shard_map/ppermute | solution.py:21
  42.9 17.7 %slice-start.1 = ((s8[10616832]{0:T(1024)(128)(4,1)}), s8[4194304]{0:T(1024)(128)(4,1)S(1)}, s32[]{:S(2)}) async-start(s8[10616832]{0:T(1024)(128)(4,1)} %bitcast.52), calls=%async_computation.2 | async-start | bytes 8388608
  43.0 17.7 %slice-start.2 = ((s8[10616832]{0:T(1024)(128)(4,1)}), s8[2228224]{0:T(1024)(128)(4,1)S(1)}, s32[]{:S(2)}) async-start(s8[10616832]{0:T(1024)(128)(4,1)} %bitcast.52), calls=%async_computation.3 | async-start | bytes 4456448
  43.0 30.1 %collective-permute-start.5 = (bf16[256,1,288]{0,2,1:T(8,128)(2,1)}, bf16[256,1,288]{0,2,1:T(8,128)(2,1)}, u32[]{:S(2)}, u32[]{:S(2)}) collective-permute-start(bf16[256,1,288]{0,2,1:T(8,128)(2,1)} %get-tuple-element.4), channel_id=1, source_target_pairs={{0,1},{1,2},{2,3},{4,5},{5,6},{6,7},{8,9},{9,10},{10,11},{12,13},{... | collective-permute-start | bytes 442376 | tf_op jit(solution)/shard_map/ppermute | solution.py:19
  73.0 21.8 %copy-start.3 = (bf16[256,8,256]{2,1,0:T(8,128)(2,1)S(1)}, bf16[256,8,256]{2,1,0:T(8,128)(2,1)}, u32[]{:S(2)}) copy-start(bf16[256,8,256]{2,1,0:T(8,128)(2,1)} %param.5) | copy-start | bytes 3145732
Sparse Core Ops, SparseCore 0:
  102.8 134.0 all-reduce.1
where the time goes:
time: 247 us
  waiting for transfers between devices  126 us (51%)
  matrix products  81 us (33%)
  starting transfers between devices  16.6 us (7%)
  between operations  14.2 us (6%)
  other arithmetic  4.73 us (2%)
  local copies, waits for them, and re-layouts  4.31 us (2%)
    psum x1, waiting for transfers between devices, local(): lax.psum(local_grad, ('lon', 'lat')) * (1.0 / math.sqrt(total_cells))  126 us
    dot_general x3, matrix products, spread_block(): jnp.einsum('oip,kipq->koiq', rows_in, tiles, preferred_element_type=jnp.f...  47.1 us
    dot_general x3, matrix products, spread_block(): jnp.einsum('bpq,kib->kipq', selector, part_coefs, preferred_element_type=...  19.8 us
    ppermute x3, starting transfers between devices, with_halo(): lax.ppermute(tail, axis, [(i, (i + 1) % count) for i in range(ends)])  10.8 us
    dot_general x1, matrix products, local(): jnp.einsum('koiq,ciq->koc', spread, inputs, preferred_element_type=jnp.fl...  7.76 us
    dot_general x1, matrix products, local(): jnp.einsum('koc,koiq->ciq', mixing, spread, preferred_element_type=jnp.fl...  6.3 us
    ppermute x3, starting transfers between devices, with_halo(): lax.ppermute(head, axis, [((i + 1) % count, i) for i in range(ends)])  5.81 us
  transfers between devices with their start and end apart: 7, of which 1 were waited for; matrix products, arithmetic and copies ran while one was open for 22% of the time, Pallas kernels for 0%

commit v1 on v0

--- a/solution.py
+++ b/solution.py
@@ -6,6 +6,11 @@
 
 LAT_REACH = 1
 LON_REACH = 16
+
+
+def add_all(x, name):
+    terms = lax.all_gather(x, name)
+    return jnp.sum(terms, axis=0)
 
 
 def with_halo(cells, sides, width, closed):
@@ -64,7 +69,7 @@
     spread = spread_block(padded, coef_pad, 0, lat_rows, 0, lon_cols)
     local_grad = jnp.einsum("koiq,ciq->koc", spread, inputs, preferred_element_type=jnp.float32)
     total_cells = lat_rows * lax.axis_size("lat") * lon_cols * lax.axis_size("lon")
-    weight_grad = lax.psum(local_grad, ("lon", "lat")) * (1.0 / math.sqrt(total_cells))
+    weight_grad = add_all(local_grad, ("lon", "lat")) * (1.0 / math.sqrt(total_cells))
     input_grad = jnp.einsum(
         "koc,koiq->ciq", mixing, spread, preferred_element_type=jnp.float32
     ).astype(jnp.bfloat16)

time: 247 us -> 532 us (2.15)
  waiting for transfers between devices: 126 us -> 389 us
  other arithmetic: 4.73 us -> 28 us
    all_gather x0 -> x1, waiting for transfers between devices: none -> 389 us  [add_all(): terms = lax.all_gather(x, name)]
    psum x1 -> x0, waiting for transfers between devices: 126 us -> none  [local(): lax.psum(local_grad, ('lon', 'lat')) * (1.0 / math.sqrt(total_cells))]
    reduce_sum x0 -> x1, other arithmetic: none -> 23.3 us  [add_all(): return jnp.sum(terms, axis=0)]
  transfers between devices with their start and end apart: 7 -> 7, of which waited for: 1 -> 1; matrix products, arithmetic and copies ran while one was open for 22% -> 11% of each run, Pallas kernels for 0% -> 0%
where the time goes in v1:
time: 532 us
  waiting for transfers between devices  389 us (73%)
  matrix products  81.3 us (15%)
  other arithmetic  28 us (5%)
  starting transfers between devices  15.8 us (3%)
  between operations  14.2 us (3%)
    all_gather x1, waiting for transfers between devices, add_all(): terms = lax.all_gather(x, name)  389 us
    dot_general x3, matrix products, spread_block(): jnp.einsum('oip,kipq->koiq', rows_in, tiles, preferred_element_type=jnp.f...  47.3 us
    reduce_sum x1, other arithmetic, add_all(): return jnp.sum(terms, axis=0)  23.3 us
    dot_general x3, matrix products, spread_block(): jnp.einsum('bpq,kib->kipq', selector, part_coefs, preferred_element_type=...  19.9 us
  transfers between devices with their start and end apart: 7, of which 1 were waited for; matrix products, arithmetic and copies ran while one was open for 11% of the time, Pallas kernels for 0%

profile of v1, /device:TPU:0, one launch (start us, length us, event | category | flops | bytes accessed | tf_op | source)
XLA Modules:
  0.0 532.0 jit_solution(11151286358783849424)
XLA Ops:
  7.2 0.0 copy-start
  7.2 0.0 all-gather.3.cloned.1.call-start
  7.2 0.8 compare_convert_fusion
  8.0 0.8 broadcast_multiply_fusion.1
  8.9 2.4 collective-permute-start.4
  11.3 1.3 collective-permute-start
  12.6 1.6 copy.13
  14.3 2.4 collective-permute-start.1
  16.6 3.1 collective-permute-start.2
  19.8 1.3 fusion.3
  21.0 6.7 %fusion.7 = bf16[9,8,288,256]{3,1,2,0:T(8,128)(2,1)} fusion(pred[33,288,256,1]{2,1,0,3:T(32,128)(4,1)S(1)} %fusion.3, bf16[9,8,3,33]{3,1,2,0:T(8,128)(2,1)S(1)} %broadcast_multiply_fusion.1), kind=kOutput, calls=%fused_computation.12 | convolution fusion | flops 350355456 | bytes 13068288 | tf_op jit(solution)/shard_map/bpq,kib->kipq/dot_general | solution.py:49
  27.7 0.0 collective-permute-done.4
  27.7 6.6 %fusion.5 = bf16[9,8,288,256]{3,1,2,0:T(8,128)(2,1)} fusion(pred[33,288,256,1]{2,1,0,3:T(32,128)(4,1)S(1)} %fusion.3, bf16[9,8,3,33]{3,1,2,0:T(8,128)(2,1)S(1)} %broadcast_multiply_fusion.1, bf16[9,1,3,33]{3,1,2,0:T(2,128)(2,1)S(1)} %collective-permute-done.4), kind=kOutput, calls=%fused_computation.10 | convolution fusion | flops 350364960 | bytes 13065894 | tf_op jit(solution)/shard_map/bpq,kib->kipq/dot_general | solution.py:49
  34.4 0.0 collective-permute-done
  34.4 6.6 %fusion.9 = bf16[9,8,288,256]{3,1,2,0:T(8,128)(2,1)} fusion(pred[33,288,256,1]{2,1,0,3:T(32,128)(4,1)S(1)} %fusion.3, bf16[9,1,3,33]{3,1,2,0:T(2,128)(2,1)S(1)} %collective-permute-done, bf16[9,8,3,33]{3,1,2,0:T(8,128)(2,1)S(1)} %broadcast_multiply_fusion.1), kind=kOutput, calls=%fused_computation.14 | convolution fusion | flops 350364960 | bytes 13065894 | tf_op jit(solution)/shard_map/bpq,kib->kipq/dot_general | solution.py:49
  40.9 0.0 collective-permute-done.1
  40.9 0.0 collective-permute-done.2
  40.9 0.1 pad_maximum_fusion.10
  41.0 0.0 slice-start
  41.0 0.7 fusion.31
  41.8 4.8 collective-permute-start.5
  46.6 0.0 slice-start.1
  46.6 0.0 slice-start.2
  46.6 1.7 collective-permute-start.3
  48.3 13.1 %fusion.1 = f32[8,9,256,256]{3,2,1,0:T(8,128)} fusion(bf16[9,8,288,256]{3,1,2,0:T(8,128)(2,1)} %fusion.7, bf16[256,8,16]{0,2,1:T(8,128)(2,1)S(1)} %collective-permute-done.2, bf16[256,8,256]{0,2,1:T(8,128)(2,1)S(1)} %copy.13, bf16[256,8,16]{0,2,1:T(8,128)(2,1)S(1)} %collective-permute-done.1), kind=kOutput, calls=%fused_computation.5 | convolution fusion | flops 2721447936 | bytes 30670848 | tf_op jit(solution)/shard_map/oip,kipq->koiq/dot_general | solution.py:52
  61.4 0.0 collective-permute-done.3
  61.4 0.0 slice-done
  61.4 0.0 slice-done.1
  61.4 0.0 slice-done.2
  61.5 12.4 %fusion = f32[8,9,256,256]{3,2,1,0:T(8,128)} fusion(bf16[9,8,288,256]{3,1,2,0:T(8,128)(2,1)S(1)} %bitcast.54, bf16[256,1,288]{0,2,1:T(8,128)(2,1)} %collective-permute-done.3, bf16[256,8,16]{0,2,1:T(8,128)(2,1)S(1)} %collective-permute-done.2, bf16[256,8,256]{0,2,1:T(8,128)(2,1)S(1)} %copy.13, bf16[256,8,16]{0,2,1:T(8,128)(2,1)S(1)} %collective-permute-done.1), kind=kOutput, calls=%fused_computation.4 | convolution fusion | flops 2722627584 | bytes 30818304 | tf_op jit(solution)/shard_map/oip,kipq->koiq/dot_general | solution.py:52
  73.8 0.0 copy-start.1
  73.8 0.0 collective-permute-done.5
  73.8 21.9 %fusion.4 = bf16[9,256,8,256]{1,3,0,2:T(8,128)(2,1)} fusion(f32[8,9,256,256]{3,2,1,0:T(8,128)} %fusion, f32[8,9,256,256]{3,2,1,0:T(8,128)} %fusion.1, bf16[9,8,288,256]{3,1,2,0:T(8,128)(2,1)} %fusion.5, bf16[256,1,288]{0,2,1:T(8,128)(2,1)} %collective-permute-done.5, bf16[256,8,16]{0,2,1:T(8,128)(2,1)S(1)} %collective-permute-done.2, ...), kind=kOutput, calls=%fused_computation.9 | convolution fusion | flops 2736783360 | bytes 59129856 | tf_op jit(solution)/shard_map/oip,kipq->koiq/dot_general | solution.py:52
  95.7 0.0 copy-done.1
  95.7 7.8 %convolution_bitcast_fusion = f32[9,256,256]{2,1,0:T(8,128)} fusion(bf16[9,256,8,256]{1,3,0,2:T(8,128)(2,1)} %fusion.4, bf16[256,8,256,1]{2,1,0,3:T(8,128)(2,1)S(1)} %bitcast.55), kind=kOutput, calls=%fused_computation.17 | convolution fusion | flops 2415919104 | bytes 12845056 | tf_op jit(solution)/shard_map/koiq,ciq->koc/dot_general | solution.py:70
  103.5 0.0 all-gather.3.cloned.1.call-update
  103.5 0.0 copy-done
  103.5 6.3 %fusion.11 = bf16[256,8,256]{0,2,1:T(8,128)(2,1)S(1)} fusion(bf16[9,256,8,256]{1,3,0,2:T(8,128)(2,1)} %fusion.4, bf16[9,256,256]{2,1,0:T(8,128)(2,1)S(1)} %copy-done), kind=kOutput, calls=%fused_computation.18 | convolution fusion | flops 2416443392 | bytes 11665408 | tf_op jit(solution)/shard_map/koc,koiq->ciq/dot_general | solution.py:73
  109.8 1.8 copy.18
  111.6 388.6 %all-gather.3.cloned.1.call-done = f32[288,256,256]{2,1,0:T(8,128)} async-done(((f32[9,256,256]{2,1,0:T(8,128)}), f32[288,256,256]{2,1,0:T(8,128)}) %all-gather.3.cloned.1.call-update) | async-done | bytes 75497488 | tf_op jit(solution)/shard_map/all_gather | solution.py:12
  500.2 23.3 %reduce_sum.9 = f32[9,256,256]{2,1,0:T(8,128)S(1)} reduce(f32[32,9,256,256]{3,2,1,0:T(8,128)} %bitcast.23, f32[]{:T(128)} %constant.3.clone.1), dimensions={0}, to_apply=%region_0.0 | reduce | flops 18284544 | bytes 77856768 | tf_op jit(solution)/shard_map/reduce_sum | solution.py:13
  523.5 1.6 broadcast_multiply_fusion
  (6 shorter events, 0.1 us)
Async XLA Ops:
  7.2 96.3 %copy-start = (bf16[9,256,256]{2,1,0:T(8,128)(2,1)S(1)}, bf16[9,256,256]{2,1,0:T(8,128)(2,1)}, u32[]{:S(2)}) copy-start(bf16[9,256,256]{2,1,0:T(8,128)(2,1)} %param.7) | copy-start | bytes 3538948
  7.2 493.0 %all-gather.3.cloned.1.call-start = ((), (), s32[]{:S(2)}) async-start(), calls=%async_computation | async-start | bytes 77856768 | tf_op jit(solution)/shard_map/all_gather | solution.py:12
  8.9 18.8 %collective-permute-start.4 = (bf16[9,1,3,33]{3,1,2,0:T(2,128)(2,1)S(1)}, bf16[9,1,3,33]{3,1,2,0:T(2,128)(2,1)S(1)}, u32[]{:S(2)}, u32[]{:S(2)}) collective-permute-start(bf16[9,1,3,33]{3,1,2,0:T(2,128)(2,1)S(1)} %get-tuple-element.10), channel_id=1, source_target_pairs={{0,1},{1,2},{2,3},{4,5},{5,6},{6,7},{8,9},{9,10},{10,11},{12,13},{... | collective-permute-start | bytes 5354 | tf_op jit(solution)/shard_map/ppermute | solution.py:24
  11.3 23.1 %collective-permute-start = (bf16[9,1,3,33]{3,1,2,0:T(2,128)(2,1)S(1)}, bf16[9,1,3,33]{3,1,2,0:T(2,128)(2,1)S(1)}, u32[]{:S(2)}, u32[]{:S(2)}) collective-permute-start(bf16[9,1,3,33]{3,1,2,0:T(2,128)(2,1)S(1)} %get-tuple-element.11), channel_id=1, source_target_pairs={{1,0},{2,1},{3,2},{5,4},{6,5},{7,6},{9,8},{10,9},{11,10},{13,12},{... | collective-permute-start | bytes 5354 | tf_op jit(solution)/shard_map/ppermute | solution.py:26
  14.3 26.7 %collective-permute-start.1 = (bf16[256,8,16]{0,2,1:T(8,128)(2,1)S(1)}, bf16[256,8,16]{0,2,1:T(8,128)(2,1)S(1)}, u32[]{:S(2)}, u32[]{:S(2)}) collective-permute-start(bf16[256,8,16]{0,2,1:T(8,128)(2,1)S(1)} %get-tuple-element.8), channel_id=1, source_target_pairs={{0,4},{4,8},{8,12},{12,16},{16,20},{20,24},{24,28},{28,0},{1,5},{5... | collective-permute-start | bytes 196616 | tf_op jit(solution)/shard_map/ppermute | solution.py:24
  16.6 24.3 %collective-permute-start.2 = (bf16[256,8,16]{0,2,1:T(8,128)(2,1)S(1)}, bf16[256,8,16]{0,2,1:T(8,128)(2,1)S(1)}, u32[]{:S(2)}, u32[]{:S(2)}) collective-permute-start(bf16[256,8,16]{0,2,1:T(8,128)(2,1)S(1)} %get-tuple-element.9), channel_id=1, source_target_pairs={{4,0},{8,4},{12,8},{16,12},{20,16},{24,20},{28,24},{0,28},{5,1},{9... | collective-permute-start | bytes 196616 | tf_op jit(solution)/shard_map/ppermute | solution.py:26
  41.0 20.4 %slice-start = ((s8[10616832]{0:T(1024)(128)(4,1)}), s8[4194304]{0:T(1024)(128)(4,1)S(1)}, s32[]{:S(2)}) async-start(s8[10616832]{0:T(1024)(128)(4,1)} %bitcast.53), calls=%async_computation.1 | async-start | bytes 8388608
  41.8 32.1 %collective-permute-start.5 = (bf16[256,1,288]{0,2,1:T(8,128)(2,1)}, bf16[256,1,288]{0,2,1:T(8,128)(2,1)}, u32[]{:S(2)}, u32[]{:S(2)}) collective-permute-start(bf16[256,1,288]{0,2,1:T(8,128)(2,1)} %get-tuple-element.6), channel_id=1, source_target_pairs={{0,1},{1,2},{2,3},{4,5},{5,6},{6,7},{8,9},{9,10},{10,11},{12,13},{... | collective-permute-start | bytes 442376 | tf_op jit(solution)/shard_map/ppermute | solution.py:24
  46.6 14.8 %slice-start.1 = ((s8[10616832]{0:T(1024)(128)(4,1)}), s8[4194304]{0:T(1024)(128)(4,1)S(1)}, s32[]{:S(2)}) async-start(s8[10616832]{0:T(1024)(128)(4,1)} %bitcast.53), calls=%async_computation.2 | async-start | bytes 8388608
  46.6 14.8 %slice-start.2 = ((s8[10616832]{0:T(1024)(128)(4,1)}), s8[2228224]{0:T(1024)(128)(4,1)S(1)}, s32[]{:S(2)}) async-start(s8[10616832]{0:T(1024)(128)(4,1)} %bitcast.53), calls=%async_computation.3 | async-start | bytes 4456448
  46.6 14.8 %collective-permute-start.3 = (bf16[256,1,288]{0,2,1:T(8,128)(2,1)}, bf16[256,1,288]{0,2,1:T(8,128)(2,1)}, u32[]{:S(2)}, u32[]{:S(2)}) collective-permute-start(bf16[256,1,288]{0,2,1:T(8,128)(2,1)} %get-tuple-element.7), channel_id=1, source_target_pairs={{1,0},{2,1},{3,2},{5,4},{6,5},{7,6},{9,8},{10,9},{11,10},{13,12},{... | collective-permute-start | bytes 442376 | tf_op jit(solution)/shard_map/ppermute | solution.py:26
  73.8 21.9 %copy-start.1 = (bf16[256,8,256]{2,1,0:T(8,128)(2,1)S(1)}, bf16[256,8,256]{2,1,0:T(8,128)(2,1)}, u32[]{:S(2)}) copy-start(bf16[256,8,256]{2,1,0:T(8,128)(2,1)} %param.5) | copy-start | bytes 3145732
Sparse Core Ops, SparseCore 0:
  103.6 396.5 all-gather.2
